TPU v7x, 256 devices: a whole 4x4x8 slice. The times are simulated.
256 devices in a mesh: replica: 4 (over x_hi, core), fsdp: 64 (over z, y, x_lo).
Axes of the slice: x: 4 (x_hi: 2, x_lo: 2; x = x_hi * 2 + x_lo), y: 4, z: 8, core: 2. Of those that a mesh axis runs over, the one named last changes fastest.
Arguments:
- deltas: bfloat16 [4, 2, 2048, 16384], P('replica', None, 'fsdp'), may hold values from -3 to 3
- master: float32 [2, 2048, 16384], P(None, 'replica', 'fsdp'), may hold values from -3 to 3
- momentum: float32 [2, 2048, 16384], P(None, 'replica', 'fsdp'), may hold values from -2 to 2
Outputs:
- master_out: float32 [2, 2048, 16384], P(None, 'replica', 'fsdp')
- momentum_out: float32 [2, 2048, 16384], P(None, 'replica', 'fsdp')
- params_out: bfloat16 [2, 2048, 16384], P(None, 'fsdp')
All inputs are finite; a program needn't handle non-finite values.
Results may differ from a plain program's by a relative error of at most 0.008.
Values may be sent and summed in bfloat16 or wider, within the bound.
No kernel may reach another device: no remote copies, remote signals or barrier semaphores. Data moves between devices by JAX's collectives and lax.ppermute only.
A program may use at most 64 MiB of HBM per device.

v0:
```python
import jax
import jax.numpy as jnp
from jax import lax
from jax.sharding import PartitionSpec as P


def split_up(value, dim, size):
    before, after = (value.shape[:dim], value.shape[dim + 1 :])
    return jnp.moveaxis(value.reshape(*before, size, -1, *after), dim, 0)


def cut_rows(length, count):
    unit = 8 if length >= 8 * count else 1
    return [length // unit * k // count * unit for k in range(1, count)]


def laid_out(blocks, dim):
    blocks = jnp.moveaxis(blocks, 0, dim)
    shape = blocks.shape
    return blocks.reshape(*shape[:dim], shape[dim] * shape[dim + 1], *shape[dim + 2 :])


def cut_exchange(value, axis, pieces, split_dim, concat_dim):
    blocks = split_up(value, split_dim, lax.axis_size(axis))
    widest = max(range(1, max(2, blocks.ndim - 1)), key=lambda d: blocks.shape[d])
    outs = []
    for slab in jnp.split(blocks, cut_rows(blocks.shape[widest], pieces), axis=widest):
        if slab.size:
            outs.append(lax.all_to_all(slab, axis, split_axis=0, concat_axis=0, tiled=True))
    return laid_out(jnp.concatenate(outs, axis=widest), concat_dim)


def summed_on_arrival(value, axis, dim):
    blocks = split_up(value, dim, lax.axis_size(axis))
    arrived = lax.all_to_all(blocks, axis, split_axis=0, concat_axis=0, tiled=True)
    return arrived.astype(jnp.float32).sum(axis=0)


def from_everyone(value, axis):
    copies = jnp.broadcast_to(value, (lax.axis_size(axis), *value.shape))
    return lax.all_to_all(copies, axis, split_axis=0, concat_axis=0, tiled=True)


def collect(value, axis, dim):
    blocks = from_everyone(value, axis)
    return laid_out(blocks, dim)


def on_device(deltas, master, momentum):
    local = deltas[0]
    groups = lax.axis_size("replica")
    moved = cut_exchange(local, "fsdp", 2, 2, 1)
    summed = summed_on_arrival(moved.astype(jnp.float32).astype(jnp.bfloat16), "replica", 1)
    outer = summed / groups
    velocity = 0.9 * momentum + outer
    updated = master - 0.7 * (outer + 0.9 * velocity)
    rounded = updated.astype(jnp.bfloat16)
    copies = collect(rounded, "replica", 1)
    spread = lax.all_to_all(copies, "fsdp", split_axis=1, concat_axis=2, tiled=True)
    return (updated, velocity, spread)


def solution(mesh):
    return jax.shard_map(
        on_device,
        mesh=mesh,
        in_specs=(
            P("replica", None, "fsdp", None),
            P(None, "replica", "fsdp"),
            P(None, "replica", "fsdp"),
        ),
        out_specs=(P(None, "replica", "fsdp"), P(None, "replica", "fsdp"), P(None, "fsdp", None)),
        check_vma=False,
    )
```

profile of v0, /device:TPU:2, one launch (start us, length us, event | category | flops | bytes accessed | tf_op | source)
XLA Modules:
  0.0 215.4 jit_solution(5978255964979203829)
XLA Ops:
  0.6 2.1 copy.19
  2.8 0.2 bitcast_bitcast_fusion
  3.0 0.1 fusion.1
  3.2 1.6 copy.8
  4.7 13.1 %all-to-all-start = ((bf16[64,2,16,256]{3,2,1,0:T(8,128)(2,1)}), bf16[64,2,16,256]{3,2,1,0:T(8,128)(2,1)S(1)}, u32[]{:S(2)}, u32[]{:S(2)}) async-start(bf16[64,2,16,256]{3,2,1,0:T(8,128)(2,1)} %copy.8), calls=%async_computation | async-start | bytes 2097152 | tf_op jit(solution)/shard_map/all_to_all | solution.py:29
  17.8 0.6 copy.9
  18.4 27.3 %all-to-all-done = bf16[64,2,16,256]{3,2,1,0:T(8,128)(2,1)S(1)} async-done(((bf16[64,2,16,256]{3,2,1,0:T(8,128)(2,1)}), bf16[64,2,16,256]{3,2,1,0:T(8,128)(2,1)S(1)}, u32[]{:S(2)}, u32[]{:S(2)}) %all-to-all-start) | async-done | bytes 1048608 | tf_op jit(solution)/shard_map/all_to_all | solution.py:29
  45.8 33.8 %all_to_all.38 = bf16[64,2,16,256]{3,2,1,0:T(8,128)(2,1)S(1)} all-to-all(bf16[64,2,16,256]{3,2,1,0:T(8,128)(2,1)S(1)} %copy.9), channel_id=1, replica_groups=mesh['replica'=4,'fsdp'=64] {'fsdp'}, dimensions={0} | all-to-all | bytes 2097152 | tf_op jit(solution)/shard_map/all_to_all | solution.py:29
  79.6 0.3 pad_maximum_fusion
  79.9 0.2 copy.17
  80.1 0.1 copy.12
  80.2 30.4 %all_to_all.39 = bf16[4,2,512,256]{3,2,1,0:T(8,128)(2,1)S(1)} all-to-all(bf16[4,2,512,256]{3,2,1,0:T(8,128)(2,1)S(1)} %copy.12), channel_id=1, replica_groups=mesh['replica'=4,'fsdp'=64] {'replica'}, dimensions={0} | all-to-all | bytes 4194304 | tf_op jit(solution)/shard_map/all_to_all | solution.py:35
  110.6 0.0 copy-start
  110.6 0.3 convert_reduce_fusion
  110.9 0.9 copy-done
  111.8 0.3 copy-done.1
  112.1 1.6 fusion
  113.7 0.1 broadcast_in_dim.3
  113.9 29.6 %all_to_all.40 = bf16[4,2,512,256]{3,2,1,0:T(8,128)(2,1)S(1)} all-to-all(bf16[4,2,512,256]{3,2,1,0:T(8,128)(2,1)S(1)} %broadcast_in_dim.3), channel_id=1, replica_groups=mesh['replica'=4,'fsdp'=64] {'replica'}, dimensions={0} | all-to-all | bytes 4194304 | tf_op jit(solution)/shard_map/all_to_all | solution.py:41
  143.5 0.1 copy.13
  143.6 12.8 %copy.14 = bf16[2,2048,256]{2,0,1:T(2,128)(2,1)S(1)} copy(bf16[2,2048,256]{2,1,0:T(8,128)(2,1)S(1)} %bitcast.23) | data formatting | bytes 4194304 | tf_op jit(solution)/shard_map/reshape | solution.py:20
  156.5 57.3 %all_to_all.41 = bf16[2,2048,256]{2,0,1:T(2,128)(2,1)S(1)} all-to-all(bf16[2,2048,256]{2,0,1:T(2,128)(2,1)S(1)} %copy.14), channel_id=1, replica_groups=mesh['replica'=4,'fsdp'=64] {'fsdp'}, dimensions={1} | all-to-all | bytes 4194304 | tf_op jit(solution)/shard_map/all_to_all | solution.py:59
  213.7 0.3 copy.15
  214.0 1.5 copy.18
  (1 shorter events, 0.0 us)
Async XLA Ops:
  4.7 41.0 %all-to-all-start = ((bf16[64,2,16,256]{3,2,1,0:T(8,128)(2,1)}), bf16[64,2,16,256]{3,2,1,0:T(8,128)(2,1)S(1)}, u32[]{:S(2)}, u32[]{:S(2)}) async-start(bf16[64,2,16,256]{3,2,1,0:T(8,128)(2,1)} %copy.8), calls=%async_computation | async-start | bytes 2097152 | tf_op jit(solution)/shard_map/all_to_all | solution.py:29
  110.6 1.2 copy-start
  110.6 1.5 copy-start.1
where the time goes:
time: 216 us; the launch traced here: 215 us
  blocking collectives  151 us (70%)
  waiting for transfers between devices  27.3 us (13%)
  local copies, waits for them, and re-layouts  21 us (10%)
  starting transfers between devices  13.1 us (6%)
  other arithmetic  2.22 us (1%)
    all_to_all x1, blocking collectives, on_device(): lax.all_to_all(copies, 'fsdp', split_axis=1, concat_axis=2, tiled=True)  57.3 us
    all_to_all x1, blocking collectives, cut_exchange(): lax.all_to_all(slab, axis, split_axis=0, concat_axis=0, tiled=True)  33.8 us
    all_to_all x1, blocking collectives, summed_on_arrival(): lax.all_to_all(blocks, axis, split_axis=0, concat_axis=0, tiled=True)  30.4 us
    all_to_all x1, blocking collectives, from_everyone(): return lax.all_to_all(copies, axis, split_axis=0, concat_axis=0, tiled=True)  29.6 us
    all_to_all x1, waiting for transfers between devices, cut_exchange(): lax.all_to_all(slab, axis, split_axis=0, concat_axis=0, tiled=True)  27.3 us
    all_to_all x1, starting transfers between devices, cut_exchange(): lax.all_to_all(slab, axis, split_axis=0, concat_axis=0, tiled=True)  13.1 us
    reshape x1, local copies, waits for them, and re-layouts, laid_out(): blocks.reshape(*shape[:dim], shape[dim] * shape[dim + 1], *shape[dim + 2:])  12.8 us
  transfers between devices with their start and end apart: 1, of which 1 were waited for; matrix products, arithmetic and copies ran while one was open for 0% of the time, Pallas kernels for 0%

commit v1 on v0

--- a/solution.py
+++ b/solution.py
@@ -56,7 +56,12 @@
     updated = master - 0.7 * (outer + 0.9 * velocity)
     rounded = updated.astype(jnp.bfloat16)
     copies = collect(rounded, "replica", 1)
-    spread = lax.all_to_all(copies, "fsdp", split_axis=1, concat_axis=2, tiled=True)
+    spread = jnp.concatenate(
+        lax.all_to_all(
+            jnp.stack(jnp.split(copies, lax.axis_size("fsdp"), axis=1), axis=0), "fsdp", 0, 0
+        ),
+        axis=2,
+    )
     return (updated, velocity, spread)
 
 

time: 216 us -> 204 us (0.944)
  local copies, waits for them, and re-layouts: 21 us -> 8.23 us
    reshape x1, local copies, waits for them, and re-layouts: 12.8 us -> 1.45 us  [on_device(): jnp.concatenate(lax.all_to_all(jnp.stack(jnp.split(copies, lax.axis_size(...]
where the time goes in v1:
time: 204 us; the launch traced here: 203 us
  blocking collectives  151 us (74%)
  waiting for transfers between devices  27.3 us (13%)
  starting transfers between devices  13.1 us (6%)
  local copies, waits for them, and re-layouts  8.23 us (4%)
  other arithmetic  2.22 us (1%)
    all_to_all x1, blocking collectives, on_device(): lax.all_to_all(jnp.stack(jnp.split(copies, lax.axis_size('fsdp'), axis=1)...  57.3 us
    all_to_all x1, blocking collectives, cut_exchange(): lax.all_to_all(slab, axis, split_axis=0, concat_axis=0, tiled=True)  33.8 us
    all_to_all x1, blocking collectives, summed_on_arrival(): lax.all_to_all(blocks, axis, split_axis=0, concat_axis=0, tiled=True)  30.4 us
    all_to_all x1, blocking collectives, from_everyone(): return lax.all_to_all(copies, axis, split_axis=0, concat_axis=0, tiled=True)  29.6 us
    all_to_all x1, waiting for transfers between devices, cut_exchange(): lax.all_to_all(slab, axis, split_axis=0, concat_axis=0, tiled=True)  27.3 us
    all_to_all x1, starting transfers between devices, cut_exchange(): lax.all_to_all(slab, axis, split_axis=0, concat_axis=0, tiled=True)  13.1 us
  transfers between devices with their start and end apart: 1, of which 1 were waited for; matrix products, arithmetic and copies ran while one was open for 0% of the time, Pallas kernels for 0%

profile of v1, /device:TPU:2, one launch (start us, length us, event | category | flops | bytes accessed | tf_op | source)
XLA Modules:
  0.0 203.2 jit_solution(8389351432701186727)
XLA Ops:
  0.6 2.1 %copy.80 = bf16[8,8,64,256]{3,2,1,0:T(8,128)(2,1)S(1)} copy(bf16[8,8,64,256]{3,1,2,0:T(8,128)(2,1)} %bitcast.343) | data formatting | bytes 4194304
  2.8 0.2 bitcast_bitcast_fusion
  3.0 0.1 fusion.1
  3.2 1.6 copy.71
  4.7 13.1 %all-to-all-start = ((bf16[64,2,16,256]{3,2,1,0:T(8,128)(2,1)}), bf16[64,2,16,256]{3,2,1,0:T(8,128)(2,1)S(1)}, u32[]{:S(2)}, u32[]{:S(2)}) async-start(bf16[64,2,16,256]{3,2,1,0:T(8,128)(2,1)} %copy.71), calls=%async_computation | async-start | bytes 2097152 | tf_op jit(solution)/shard_map/all_to_all | solution.py:29
  17.8 0.6 copy.72
  18.4 27.3 %all-to-all-done = bf16[64,2,16,256]{3,2,1,0:T(8,128)(2,1)S(1)} async-done(((bf16[64,2,16,256]{3,2,1,0:T(8,128)(2,1)}), bf16[64,2,16,256]{3,2,1,0:T(8,128)(2,1)S(1)}, u32[]{:S(2)}, u32[]{:S(2)}) %all-to-all-start) | async-done | bytes 1048608 | tf_op jit(solution)/shard_map/all_to_all | solution.py:29
  45.8 33.8 %all_to_all.25 = bf16[64,2,16,256]{3,2,1,0:T(8,128)(2,1)S(1)} all-to-all(bf16[64,2,16,256]{3,2,1,0:T(8,128)(2,1)S(1)} %copy.72), channel_id=1, replica_groups=mesh['replica'=4,'fsdp'=64] {'fsdp'}, dimensions={0} | all-to-all | bytes 2097152 | tf_op jit(solution)/shard_map/all_to_all | solution.py:29
  79.6 0.3 pad_maximum_fusion
  79.9 0.2 copy.78
  80.1 0.1 copy.75
  80.2 30.4 %all_to_all.26 = bf16[4,2,512,256]{3,2,1,0:T(8,128)(2,1)S(1)} all-to-all(bf16[4,2,512,256]{3,2,1,0:T(8,128)(2,1)S(1)} %copy.75), channel_id=1, replica_groups=mesh['replica'=4,'fsdp'=64] {'replica'}, dimensions={0} | all-to-all | bytes 4194304 | tf_op jit(solution)/shard_map/all_to_all | solution.py:35
  110.6 0.0 copy-start
  110.6 0.0 copy-start.1
  110.6 0.3 convert_reduce_fusion
  110.9 0.9 copy-done
  111.8 0.3 copy-done.1
  112.1 1.6 fusion
  113.7 0.1 broadcast_in_dim.3
  113.9 29.6 %all_to_all.27 = bf16[4,2,512,256]{3,2,1,0:T(8,128)(2,1)S(1)} all-to-all(bf16[4,2,512,256]{3,2,1,0:T(8,128)(2,1)S(1)} %broadcast_in_dim.3), channel_id=1, replica_groups=mesh['replica'=4,'fsdp'=64] {'replica'}, dimensions={0} | all-to-all | bytes 4194304 | tf_op jit(solution)/shard_map/all_to_all | solution.py:41
  143.5 0.1 copy.76
  144.5 57.3 %all_to_all.28 = bf16[64,2,32,256]{3,2,1,0:T(8,128)(2,1)S(1)} all-to-all(bf16[64,2,32,256]{3,2,1,0:T(8,128)(2,1)S(1)} %constant_dynamic-update-slice_fusion), channel_id=1, replica_groups=mesh['replica'=4,'fsdp'=64] {'fsdp'}, dimensions={0} | all-to-all | bytes 4194304 | tf_op jit(solution)/shard_map/all_to_all | solution.py:60
  201.7 1.5 copy.79
  (64 shorter events, 0.3 us)
Async XLA Ops:
  4.7 41.0 %all-to-all-start = ((bf16[64,2,16,256]{3,2,1,0:T(8,128)(2,1)}), bf16[64,2,16,256]{3,2,1,0:T(8,128)(2,1)S(1)}, u32[]{:S(2)}, u32[]{:S(2)}) async-start(bf16[64,2,16,256]{3,2,1,0:T(8,128)(2,1)} %copy.71), calls=%async_computation | async-start | bytes 2097152 | tf_op jit(solution)/shard_map/all_to_all | solution.py:29
  110.6 1.2 copy-start
  110.6 1.5 copy-start.1
